TPU v7x, 128 devices: a whole 4x4x4 slice. The times are simulated.
128 devices in a mesh: prompt: 4 (over z_hi, core), resp: 32 (over y, x, z_lo).
Axes of the slice: x: 4, y: 4, z: 4 (z_hi: 2, z_lo: 2; z = z_hi * 2 + z_lo), core: 2. Of those that a mesh axis runs over, the one named last changes fastest.
Arguments:
- queries: bfloat16 [4, 4096, 8192], P('prompt', 'resp'), may hold values from -6 to 6
- resp_kv: bfloat16 [4, 4096, 2048], P('prompt', 'resp'), may hold values from -6 to 6
- resp_segments: int32 [4, 4096], P('prompt', 'resp'), may hold values from 0 to 7, never falling along the last dimension, each value on 1 to 896 neighbouring positions
- prefix_kv: bfloat16 [512, 8, 2048], P(('prompt', 'resp')), may hold values from -6 to 6
- tile_plan: int32 [512, 2], P(('prompt', 'resp')), may hold values from 0 to 127, as said below
- prompt_lengths: int32 [4], P('prompt'), may hold values from 8 to 1024
Outputs:
- attended: bfloat16 [4, 4096, 8192], P('prompt', 'resp')
Inputs may be any that keep to these rules, and one draw needn't show every extreme that they name: `tile_plan`: column 0 is a group in 0 .. 3 and column 1 a place in 0 .. 127; each pair of group and place stands once; the 4 tiles of each device hold one tile of every group, in any order. `resp_segments`: response numbers never fall along a group's tokens; each response has 1 to 896 tokens.
All inputs are finite; a program needn't handle non-finite values.
Results may differ from a plain program's by a relative error of at most 0.0055.
Values may be sent and summed in bfloat16 or wider, within the bound.
A program may use at most 128 MiB of HBM per device.

v0:
```python
import math
import jax
import jax.numpy as jnp
from jax import lax
from jax.sharding import PartitionSpec as P

H = 64
KVH = 8
HD = 128
NEG_FILL = -1e30


def passed_along(value, axis, steps):
    count = lax.axis_size(axis)
    first, last = (max(0, -steps), min(count, count - steps))
    return lax.ppermute(value, axis, [(source, source + steps) for source in range(first, last)])


def absorb(carry, query_head_rows, key_vectors, value_vectors, visible, score_scale):
    running, total, weighted_sum = carry
    logit_scores = (
        jnp.einsum(
            "wcpo,lco->wcpl", query_head_rows, key_vectors, preferred_element_type=jnp.float32
        )
        * score_scale
    )
    logit_scores = jnp.where(visible, logit_scores, NEG_FILL)
    fresh = jnp.maximum(running, jnp.max(logit_scores, axis=-1))
    factor = jnp.exp(running - fresh)
    attention_weight = jnp.where(visible, jnp.exp(logit_scores - fresh[..., None]), 0.0)
    total = total * factor + jnp.sum(attention_weight, axis=-1)
    update = jnp.einsum(
        "luem,mut->luet",
        attention_weight.astype(jnp.bfloat16),
        value_vectors,
        preferred_element_type=jnp.float32,
    )
    weighted_sum = weighted_sum * factor[..., None] + update
    return (fresh, total, weighted_sum)


def on_device(queries, resp_kv, resp_segments, prefix_kv, tile_plan, prompt_lengths):
    rows = queries.shape[1]
    heads_kv = KVH
    width = HD
    group_size = H // KVH
    split = heads_kv * width
    score_scale = 1.0 / math.sqrt(width)
    reach = 7
    query_head_rows = queries[0].reshape(rows, heads_kv, group_size, width)
    own_kv = resp_kv[0]
    own_seg = resp_segments[0] + 1
    key_vectors = own_kv[:, :split].reshape(rows, heads_kv, width)
    value_vectors = own_kv[:, split:].reshape(rows, heads_kv, width)
    query_pos = jnp.arange(rows, dtype=jnp.int32)
    visible = (own_seg[None, :] == own_seg[:, None]) & (query_pos[None, :] <= query_pos[:, None])
    start_state = (
        jnp.full((rows, heads_kv, group_size), NEG_FILL, jnp.float32),
        jnp.zeros((rows, heads_kv, group_size), jnp.float32),
        jnp.zeros((rows, heads_kv, group_size, width), jnp.float32),
    )
    carry = absorb(
        start_state,
        query_head_rows,
        key_vectors,
        value_vectors,
        visible[:, None, None, :],
        score_scale,
    )
    moving = (own_kv, own_seg)
    for step in range(reach):
        moving = passed_along((moving[0], moving[1]), "resp", 1)
        block_kv = moving[0]
        seen = own_seg[:, None] == moving[1][None, :]

        def absorb_update(current):
            block_keys = block_kv[:, :split].reshape(-1, heads_kv, width)
            block_values = block_kv[:, split:].reshape(-1, heads_kv, width)
            return absorb(
                current,
                query_head_rows,
                block_keys,
                block_values,
                seen[:, None, None, :],
                score_scale,
            )

        carry = lax.cond(jnp.any(seen), absorb_update, lambda current: current, carry)
    group = lax.axis_index("prompt")
    limit = prompt_lengths[0]
    n_prompt = lax.axis_size("prompt")
    state = carry
    tiles = lax.all_gather(prefix_kv, ("prompt", "resp"), axis=0, tiled=True)
    plan = lax.all_gather(tile_plan, ("prompt", "resp"), axis=0, tiled=True)
    count = tiles.shape[0]
    tile = tiles.shape[1]
    count = count // n_prompt
    order = jnp.argsort(jnp.where(plan[:, 0] == group, 0, 1), stable=True)[:count]
    tiles = tiles[order]
    plan = plan[order]
    cap = max(1, 512 // tile)
    per = max((d for d in range(1, min(count, cap) + 1) if count % d == 0))
    places = plan[:, 1][:, None] * tile + jnp.arange(tile, dtype=jnp.int32)[None, :]
    live = (places < limit).reshape(count // per, per * tile)
    blocks = tiles.reshape(count // per, per * tile, tiles.shape[2])

    def advance(inner, item):
        block, mask = item

        def update(current):
            block_keys = block[:, :split].reshape(-1, heads_kv, width)
            block_values = block[:, split:].reshape(-1, heads_kv, width)
            return absorb(
                current,
                query_head_rows,
                block_keys,
                block_values,
                mask[None, None, None, :],
                score_scale,
            )

        return (lax.cond(jnp.any(mask), update, lambda current: current, inner), None)

    state, _ = lax.scan(advance, state, (blocks, live))
    carry = state
    running, total, weighted_sum = carry
    result = (weighted_sum / total[..., None]).reshape(rows, H * HD).astype(jnp.bfloat16)
    return result[None]


def solution(mesh):
    return jax.shard_map(
        on_device,
        mesh=mesh,
        in_specs=(
            P("prompt", "resp", None),
            P("prompt", "resp", None),
            P("prompt", "resp"),
            P(("prompt", "resp"), None, None),
            P(("prompt", "resp"), None),
            P("prompt"),
        ),
        out_specs=P("prompt", "resp", None),
        check_vma=False,
    )
```

profile of v0, /device:TPU:89, one launch (start us, length us, event | category | flops | bytes accessed | tf_op | source)
XLA Modules:
  0.0 580.5 jit_solution(3379956316032789623)
XLA Ops:
  11.8 14.5 %collective-permute-done.7 = bf16[128,2048]{0,1:T(8,128)(2,1)S(1)} collective-permute-done((bf16[128,2048]{0,1:T(8,128)(2,1)S(1)}, bf16[128,2048]{0,1:T(8,128)(2,1)S(1)}, u32[]{:S(2)}, u32[]{:S(2)}) %collective-permute-start.7) | collective-permute-done | bytes 524320 | tf_op jit(solution)/shard_map/ppermute | solution.py:16
  28.2 14.9 %collective-permute-done.8 = bf16[128,2048]{0,1:T(8,128)(2,1)S(1)} collective-permute-done((bf16[128,2048]{0,1:T(8,128)(2,1)S(1)}, bf16[128,2048]{0,1:T(8,128)(2,1)S(1)}, u32[]{:S(2)}, u32[]{:S(2)}) %collective-permute-start.8) | collective-permute-done | bytes 524320 | tf_op jit(solution)/shard_map/ppermute | solution.py:16
  51.0 8.1 %collective-permute-done = s32[128]{0:T(128)S(1)} collective-permute-done((s32[128]{0:T(128)S(1)}, s32[128]{0:T(128)S(1)}, u32[]{:S(2)}, u32[]{:S(2)}) %collective-permute-start) | collective-permute-done | bytes 544 | tf_op jit(solution)/shard_map/ppermute | solution.py:16
  61.4 291.9 %all-gather = s32[128,4,2]{1,2,0:T(2,128)S(1)} all-gather(s32[1,4,2]{1,2,0:T(2,128)} %bitcast.282), channel_id=1, replica_groups=mesh['prompt'=4,'resp'=32] {'prompt','resp'}, dimensions={0}, use_global_device_ids=true | all-gather | bytes 4128 | tf_op jit(solution)/shard_map/all_gather | solution.py:94
  361.7 7.3 %collective-permute-start.3 = (s32[128]{0:T(128)S(1)}, s32[128]{0:T(128)S(1)}, u32[]{:S(2)}, u32[]{:S(2)}) collective-permute-start(s32[128]{0:T(128)S(1)} %collective-permute-done.2), channel_id=1, source_target_pairs={{0,1},{1,2},{2,3},{3,4},{4,5},{5,6},{6,7},{7,8},{8,9},{9,10},{10,1... | collective-permute-start | bytes 1544 | tf_op jit(solution)/shard_map/ppermute | solution.py:16
  372.7 7.5 %collective-permute-start.4 = (s32[128]{0:T(128)S(1)}, s32[128]{0:T(128)S(1)}, u32[]{:S(2)}, u32[]{:S(2)}) collective-permute-start(s32[128]{0:T(128)S(1)} %collective-permute-done.3), channel_id=1, source_target_pairs={{0,1},{1,2},{2,3},{3,4},{4,5},{5,6},{6,7},{7,8},{8,9},{9,10},{10,1... | collective-permute-start | bytes 1544 | tf_op jit(solution)/shard_map/ppermute | solution.py:16
  383.1 6.0 %collective-permute-start.5 = (s32[128]{0:T(128)S(1)}, s32[128]{0:T(128)S(1)}, u32[]{:S(2)}, u32[]{:S(2)}) collective-permute-start(s32[128]{0:T(128)S(1)} %collective-permute-done.4), channel_id=1, source_target_pairs={{0,1},{1,2},{2,3},{3,4},{4,5},{5,6},{6,7},{7,8},{8,9},{9,10},{10,1... | collective-permute-start | bytes 1544 | tf_op jit(solution)/shard_map/ppermute | solution.py:16
  409.1 9.0 %collective-permute-done.11 = bf16[128,2048]{0,1:T(8,128)(2,1)S(1)} collective-permute-done((bf16[128,2048]{0,1:T(8,128)(2,1)}, bf16[128,2048]{0,1:T(8,128)(2,1)S(1)}, u32[]{:S(2)}, u32[]{:S(2)}) %collective-permute-start.11) | collective-permute-done | bytes 524320 | tf_op jit(solution)/shard_map/ppermute | solution.py:16
  423.7 7.5 %collective-permute-done.12 = bf16[128,2048]{0,1:T(8,128)(2,1)} collective-permute-done((bf16[128,2048]{0,1:T(8,128)(2,1)S(1)}, bf16[128,2048]{0,1:T(8,128)(2,1)}, u32[]{:S(2)}, u32[]{:S(2)}) %collective-permute-start.12) | collective-permute-done | bytes 524320 | tf_op jit(solution)/shard_map/ppermute | solution.py:16
  437.5 5.3 bitcast_add_fusion.8
  442.8 8.4 %conditional.8 = ((f32[128,8,8]{0,2,1:T(8,128)S(1)}, f32[128,8,8]{0,2,1:T(8,128)S(1)}, f32[128,8,8,128]{3,0,2,1:T(8,128)})) conditional(s32[]{:T(128)} %convert_element_type.71, (f32[128,8,8]{0,2,1:T(8,128)S(1)}, f32[128,8,8]{0,2,1:T(8,128)S(1)}, f32[128,8,8,128]{3,0,2,1:T(8,128)}) %tuple.61, (pred[128,128]{0,1:T(8,128)(4,1)S(1)}, ...), branch_computations={%region_9.10_spmd, %region_10.13_spmd} | conditional | flops 552615936 | bytes 25215008 | solution.py:88
  451.2 8.9 %conditional.9 = ((f32[128,8,8]{0,2,1:T(8,128)S(1)}, f32[128,8,8]{0,2,1:T(8,128)S(1)}, f32[128,8,8,128]{3,0,2,1:T(8,128)})) conditional(s32[]{:T(128)} %convert_element_type.70, (f32[128,8,8]{0,2,1:T(8,128)S(1)}, f32[128,8,8]{0,2,1:T(8,128)S(1)}, f32[128,8,8,128]{3,0,2,1:T(8,128)}) %get-tuple-element.662, (pred[128,128]{0,1:T(8,128)(4,1)S(1)}, ...), branch_computations={%region_13.14_spmd, %region_14.17_spmd} | conditional | flops 552615936 | bytes 25215008 | solution.py:88
  460.1 7.4 %conditional.10 = ((f32[128,8,8]{0,2,1:T(8,128)S(1)}, f32[128,8,8]{0,2,1:T(8,128)S(1)}, f32[128,8,8,128]{3,0,2,1:T(8,128)})) conditional(s32[]{:T(128)} %convert_element_type.69, (f32[128,8,8]{0,2,1:T(8,128)S(1)}, f32[128,8,8]{0,2,1:T(8,128)S(1)}, f32[128,8,8,128]{3,0,2,1:T(8,128)}) %get-tuple-element.663, (pred[128,128]{0,1:T(8,128)(4,1)S(1)}, ...), branch_computations={%region_17.18_spmd, %region_18.21_spmd} | conditional | flops 552615936 | bytes 25215008 | solution.py:88
  467.5 8.5 %conditional.11 = ((f32[128,8,8]{0,2,1:T(8,128)S(1)}, f32[128,8,8]{0,2,1:T(8,128)S(1)}, f32[128,8,8,128]{3,0,2,1:T(8,128)})) conditional(s32[]{:T(128)} %convert_element_type.68, (f32[128,8,8]{0,2,1:T(8,128)S(1)}, f32[128,8,8]{0,2,1:T(8,128)S(1)}, f32[128,8,8,128]{3,0,2,1:T(8,128)}) %get-tuple-element.664, (pred[128,128]{0,1:T(8,128)(4,1)S(1)}, ...), branch_computations={%region_21.0_spmd, %region_22.25_spmd} | conditional | flops 552615936 | bytes 25215008 | solution.py:88
  476.0 7.6 %conditional.12 = ((f32[128,8,8]{0,2,1:T(8,128)S(1)}, f32[128,8,8]{0,2,1:T(8,128)S(1)}, f32[128,8,8,128]{3,0,2,1:T(8,128)})) conditional(s32[]{:T(128)} %convert_element_type.67, (f32[128,8,8]{0,2,1:T(8,128)S(1)}, f32[128,8,8]{0,2,1:T(8,128)S(1)}, f32[128,8,8,128]{3,0,2,1:T(8,128)}) %get-tuple-element.665, (pred[128,128]{0,1:T(8,128)(4,1)S(1)}, ...), branch_computations={%region_25.0_spmd, %region_26.29_spmd} | conditional | flops 552615936 | bytes 25215008 | solution.py:88
  483.6 8.4 %conditional.13 = ((f32[128,8,8]{0,2,1:T(8,128)S(1)}, f32[128,8,8]{0,2,1:T(8,128)S(1)}, f32[128,8,8,128]{3,0,2,1:T(8,128)})) conditional(s32[]{:T(128)} %convert_element_type.66, (f32[128,8,8]{0,2,1:T(8,128)S(1)}, f32[128,8,8]{0,2,1:T(8,128)S(1)}, f32[128,8,8,128]{3,0,2,1:T(8,128)}) %get-tuple-element.666, (pred[128,128]{0,1:T(8,128)(4,1)S(1)}, ...), branch_computations={%region_29.30_spmd, %region_30.33_spmd} | conditional | flops 552615936 | bytes 25215008 | solution.py:88
  492.0 7.6 %conditional.14 = ((f32[128,8,8]{0,2,1:T(8,128)S(1)}, f32[128,8,8]{0,2,1:T(8,128)S(1)}, f32[128,8,8,128]{3,0,2,1:T(8,128)})) conditional(s32[]{:T(128)} %convert_element_type.65, (f32[128,8,8]{0,2,1:T(8,128)S(1)}, f32[128,8,8]{0,2,1:T(8,128)S(1)}, f32[128,8,8,128]{3,0,2,1:T(8,128)}) %get-tuple-element.667, (pred[128,128]{0,1:T(8,128)(4,1)S(1)}, ...), branch_computations={%region_33.34_spmd, %region_34.37_spmd} | conditional | flops 552615936 | bytes 25215008 | solution.py:88
  499.6 8.6 %gather_fusion.1 = bf16[128,8,2048]{2,1,0:T(8,128)(2,1)} fusion(bf16[512,8,2048]{2,1,0:T(8,128)(2,1)} %all-gather.3.cloned.1.call-done, s32[1024]{0:T(1024)S(1)} %pad_clamp_fusion), kind=kCustom, calls=%fused_computation.1 | custom fusion | bytes 8389120 | tf_op jit(solution)/shard_map/gather | solution.py:99
  508.2 6.4 %copy.137 = bf16[2,512,2048]{1,2,0:T(8,128)(2,1)} copy(bf16[2,512,2048]{2,1,0:T(8,128)(2,1)} %bitcast.261) | data formatting | bytes 8388608 | tf_op jit(solution)/shard_map/while | solution.py:124
  514.6 49.1 %while.14 = (s32[]{:T(128)}, f32[128,8,8]{0,2,1:T(8,128)S(1)}, f32[128,8,8]{0,2,1:T(8,128)S(1)}, f32[128,8,8,128]{3,0,2,1:T(8,128)}, pred[2,512]{1,0:T(4,128)(4,...) while((s32[]{:T(128)}, f32[128,8,8]{0,2,1:T(8,128)S(1)}, ...), condition=%wide.region_44.45_spmd, body=%wide.region_38.44_spmd.sunk | while | flops 2204123648 | bytes 138940144 | solution.py:124
  515.9 23.3 %conditional.16 = ((f32[128,8,8]{0,2,1:T(8,128)S(1)}, f32[128,8,8]{0,2,1:T(8,128)S(1)}, f32[128,8,8,128]{3,0,2,1:T(8,128)})) conditional(s32[]{:T(128)} %convert_element_type.97, (f32[128,8,8]{0,2,1:T(8,128)S(1)}, f32[128,8,8]{0,2,1:T(8,128)S(1)}, f32[128,8,8,128]{3,0,2,1:T(8,128)}) %tuple.148, (pred[1,512]{1,0:T(4,128)(4,1)S(1)}, ...), branch_computations={%region_40.40_spmd, %region_41.43_spmd} | conditional | flops 2204123136 | bytes 138938944 | solution.py:122
  527.6 11.6 %bitcast_add_fusion.7 = f32[128,8,8,128]{3,0,2,1:T(8,128)} fusion(f32[128,8,8,128]{3,0,2,1:T(8,128)} %get-tuple-element.245, bf16[512,8,128,1]{0,2,3,1:T(8,128)(2,1)S(1)} %bitcast.260, f32[8,512,128,8]{2,1,3,0:T(8,128)} %copy-done, f32[128,8,8]{0,2,1:T(8,128)S(1)} %max.24, pred[512]{0:T(512)(128)(4,1)S(1)} %reduce.1, f32[128,8,8]{0,2,1:T(8,128)S(1)} %get-tuple-element.488), kind=kOutput, calls=%fused_computation.124 | convolution fusion | flops 1096810496 | bytes 26280448 | tf_op jit(solution)/shard_map/while/body/eval_jaxpr/cond/branch_1_fun/luem,mut->luet/dot_general | solution.py:32
  540.4 23.3 %conditional.16 = ((f32[128,8,8]{0,2,1:T(8,128)S(1)}, f32[128,8,8]{0,2,1:T(8,128)S(1)}, f32[128,8,8,128]{3,0,2,1:T(8,128)})) conditional(s32[]{:T(128)} %convert_element_type.97, (f32[128,8,8]{0,2,1:T(8,128)S(1)}, f32[128,8,8]{0,2,1:T(8,128)S(1)}, f32[128,8,8,128]{3,0,2,1:T(8,128)}) %tuple.148, (pred[1,512]{1,0:T(4,128)(4,1)S(1)}, ...), branch_computations={%region_40.40_spmd, %region_41.43_spmd} | conditional | flops 2204123136 | bytes 138938944 | solution.py:122
  552.2 11.6 %bitcast_add_fusion.7 = f32[128,8,8,128]{3,0,2,1:T(8,128)} fusion(f32[128,8,8,128]{3,0,2,1:T(8,128)} %get-tuple-element.245, bf16[512,8,128,1]{0,2,3,1:T(8,128)(2,1)S(1)} %bitcast.260, f32[8,512,128,8]{2,1,3,0:T(8,128)} %copy-done, f32[128,8,8]{0,2,1:T(8,128)S(1)} %max.24, pred[512]{0:T(512)(128)(4,1)S(1)} %reduce.1, f32[128,8,8]{0,2,1:T(8,128)S(1)} %get-tuple-element.488), kind=kOutput, calls=%fused_computation.124 | convolution fusion | flops 1096810496 | bytes 26280448 | tf_op jit(solution)/shard_map/while/body/eval_jaxpr/cond/branch_1_fun/luem,mut->luet/dot_general | solution.py:32
  (131 shorter events, 148.9 us)
Async XLA Ops:
  6.5 493.1 %all-gather.3.cloned.1.call-start = ((), (), s32[]{:S(2)}) async-start(), calls=%async_computation | async-start | bytes 16908288 | tf_op jit(solution)/shard_map/all_gather | solution.py:93
  8.6 17.8 %collective-permute-start.7 = (bf16[128,2048]{0,1:T(8,128)(2,1)S(1)}, bf16[128,2048]{0,1:T(8,128)(2,1)S(1)}, u32[]{:S(2)}, u32[]{:S(2)}) collective-permute-start(bf16[128,2048]{0,1:T(8,128)(2,1)S(1)} %bitcast.264), channel_id=1, source_target_pairs={{0,1},{1,2},{2,3},{3,4},{4,5},{5,6},{6,7},{7,8},{8,9},{9,10},{10,1... | collective-permute-start | bytes 1572872 | tf_op jit(solution)/shard_map/ppermute | solution.py:16
  26.3 368.8 %copy-start.5 = (bf16[128,2048]{0,1:T(8,128)(2,1)}, bf16[128,2048]{0,1:T(8,128)(2,1)S(1)}, u32[]{:S(2)}) copy-start(bf16[128,2048]{0,1:T(8,128)(2,1)S(1)} %collective-permute-done.7) | copy-start | bytes 1572868
  26.3 16.8 %collective-permute-start.8 = (bf16[128,2048]{0,1:T(8,128)(2,1)S(1)}, bf16[128,2048]{0,1:T(8,128)(2,1)S(1)}, u32[]{:S(2)}, u32[]{:S(2)}) collective-permute-start(bf16[128,2048]{0,1:T(8,128)(2,1)S(1)} %collective-permute-done.7), channel_id=1, source_target_pairs={{0,1},{1,2},{2,3},{3,4},{4,5},{5,6},{6,7},{7,8},{8,9},{9,10},{10,1... | collective-permute-start | bytes 1572872 | tf_op jit(solution)/shard_map/ppermute | solution.py:16
  43.2 352.0 %copy-start.4 = (bf16[128,2048]{0,1:T(8,128)(2,1)}, bf16[128,2048]{0,1:T(8,128)(2,1)S(1)}, u32[]{:S(2)}) copy-start(bf16[128,2048]{0,1:T(8,128)(2,1)S(1)} %collective-permute-done.8) | copy-start | bytes 1572868
  43.2 325.9 %collective-permute-start.9 = (bf16[128,2048]{0,1:T(8,128)(2,1)S(1)}, bf16[128,2048]{0,1:T(8,128)(2,1)S(1)}, u32[]{:S(2)}, u32[]{:S(2)}) collective-permute-start(bf16[128,2048]{0,1:T(8,128)(2,1)S(1)} %collective-permute-done.8), channel_id=1, source_target_pairs={{0,1},{1,2},{2,3},{3,4},{4,5},{5,6},{6,7},{7,8},{8,9},{9,10},{10,1... | collective-permute-start | bytes 1572872 | tf_op jit(solution)/shard_map/ppermute | solution.py:16
  45.7 13.4 %collective-permute-start = (s32[128]{0:T(128)S(1)}, s32[128]{0:T(128)S(1)}, u32[]{:S(2)}, u32[]{:S(2)}) collective-permute-start(s32[128]{0:T(128)S(1)} %add_bitcast_fusion), channel_id=1, source_target_pairs={{0,1},{1,2},{2,3},{3,4},{4,5},{5,6},{6,7},{7,8},{8,9},{9,10},{10,1... | collective-permute-start | bytes 1544 | tf_op jit(solution)/shard_map/ppermute | solution.py:16
  59.1 295.0 %collective-permute-start.1 = (s32[128]{0:T(128)S(1)}, s32[128]{0:T(128)S(1)}, u32[]{:S(2)}, u32[]{:S(2)}) collective-permute-start(s32[128]{0:T(128)S(1)} %collective-permute-done), channel_id=1, source_target_pairs={{0,1},{1,2},{2,3},{3,4},{4,5},{5,6},{6,7},{7,8},{8,9},{9,10},{10,1... | collective-permute-start | bytes 1544 | tf_op jit(solution)/shard_map/ppermute | solution.py:16
  354.2 7.5 %collective-permute-start.2 = (s32[128]{0:T(128)S(1)}, s32[128]{0:T(128)S(1)}, u32[]{:S(2)}, u32[]{:S(2)}) collective-permute-start(s32[128]{0:T(128)S(1)} %collective-permute-done.1), channel_id=1, source_target_pairs={{0,1},{1,2},{2,3},{3,4},{4,5},{5,6},{6,7},{7,8},{8,9},{9,10},{10,1... | collective-permute-start | bytes 1544 | tf_op jit(solution)/shard_map/ppermute | solution.py:16
  361.7 11.0 %collective-permute-start.3 = (s32[128]{0:T(128)S(1)}, s32[128]{0:T(128)S(1)}, u32[]{:S(2)}, u32[]{:S(2)}) collective-permute-start(s32[128]{0:T(128)S(1)} %collective-permute-done.2), channel_id=1, source_target_pairs={{0,1},{1,2},{2,3},{3,4},{4,5},{5,6},{6,7},{7,8},{8,9},{9,10},{10,1... | collective-permute-start | bytes 1544 | tf_op jit(solution)/shard_map/ppermute | solution.py:16
  369.1 32.0 %collective-permute-start.10 = (bf16[128,2048]{0,1:T(8,128)(2,1)S(1)}, bf16[128,2048]{0,1:T(8,128)(2,1)}, u32[]{:S(2)}, u32[]{:S(2)}) collective-permute-start(bf16[128,2048]{0,1:T(8,128)(2,1)S(1)} %collective-permute-done.9), channel_id=1, source_target_pairs={{0,1},{1,2},{2,3},{3,4},{4,5},{5,6},{6,7},{7,8},{8,9},{9,10},{10,1... | collective-permute-start | bytes 1572872 | tf_op jit(solution)/shard_map/ppermute | solution.py:16
  372.7 10.4 %collective-permute-start.4 = (s32[128]{0:T(128)S(1)}, s32[128]{0:T(128)S(1)}, u32[]{:S(2)}, u32[]{:S(2)}) collective-permute-start(s32[128]{0:T(128)S(1)} %collective-permute-done.3), channel_id=1, source_target_pairs={{0,1},{1,2},{2,3},{3,4},{4,5},{5,6},{6,7},{7,8},{8,9},{9,10},{10,1... | collective-permute-start | bytes 1544 | tf_op jit(solution)/shard_map/ppermute | solution.py:16
  383.1 7.3 %collective-permute-start.5 = (s32[128]{0:T(128)S(1)}, s32[128]{0:T(128)S(1)}, u32[]{:S(2)}, u32[]{:S(2)}) collective-permute-start(s32[128]{0:T(128)S(1)} %collective-permute-done.4), channel_id=1, source_target_pairs={{0,1},{1,2},{2,3},{3,4},{4,5},{5,6},{6,7},{7,8},{8,9},{9,10},{10,1... | collective-permute-start | bytes 1544 | tf_op jit(solution)/shard_map/ppermute | solution.py:16
  390.4 15.0 %collective-permute-start.6 = (s32[128]{0:T(128)S(1)}, s32[128]{0:T(128)S(1)}, u32[]{:S(2)}, u32[]{:S(2)}) collective-permute-start(s32[128]{0:T(128)S(1)} %collective-permute-done.5), channel_id=1, source_target_pairs={{0,1},{1,2},{2,3},{3,4},{4,5},{5,6},{6,7},{7,8},{8,9},{9,10},{10,1... | collective-permute-start | bytes 1544 | tf_op jit(solution)/shard_map/ppermute | solution.py:16
  401.0 17.1 %collective-permute-start.11 = (bf16[128,2048]{0,1:T(8,128)(2,1)}, bf16[128,2048]{0,1:T(8,128)(2,1)S(1)}, u32[]{:S(2)}, u32[]{:S(2)}) collective-permute-start(bf16[128,2048]{0,1:T(8,128)(2,1)} %collective-permute-done.10), channel_id=1, source_target_pairs={{0,1},{1,2},{2,3},{3,4},{4,5},{5,6},{6,7},{7,8},{8,9},{9,10},{10,1... | collective-permute-start | bytes 1572872 | tf_op jit(solution)/shard_map/ppermute | solution.py:16
  418.1 13.0 %copy-start.2 = (bf16[128,2048]{0,1:T(8,128)(2,1)}, bf16[128,2048]{0,1:T(8,128)(2,1)S(1)}, u32[]{:S(2)}) copy-start(bf16[128,2048]{0,1:T(8,128)(2,1)S(1)} %collective-permute-done.11) | copy-start | bytes 1572868
  418.1 13.0 %collective-permute-start.12 = (bf16[128,2048]{0,1:T(8,128)(2,1)S(1)}, bf16[128,2048]{0,1:T(8,128)(2,1)}, u32[]{:S(2)}, u32[]{:S(2)}) collective-permute-start(bf16[128,2048]{0,1:T(8,128)(2,1)S(1)} %collective-permute-done.11), channel_id=1, source_target_pairs={{0,1},{1,2},{2,3},{3,4},{4,5},{5,6},{6,7},{7,8},{8,9},{9,10},{10,1... | collective-permute-start | bytes 1572872 | tf_op jit(solution)/shard_map/ppermute | solution.py:16
  431.2 60.8 %collective-permute-start.13 = (bf16[128,2048]{0,1:T(8,128)(2,1)}, bf16[128,2048]{0,1:T(8,128)(2,1)S(1)}, u32[]{:S(2)}, u32[]{:S(2)}) collective-permute-start(bf16[128,2048]{0,1:T(8,128)(2,1)} %collective-permute-done.12), channel_id=1, source_target_pairs={{0,1},{1,2},{2,3},{3,4},{4,5},{5,6},{6,7},{7,8},{8,9},{9,10},{10,1... | collective-permute-start | bytes 1572872 | tf_op jit(solution)/shard_map/ppermute | solution.py:16
  467.5 8.5 %copy-start.3 = (bf16[128,2048]{0,1:T(8,128)(2,1)S(1)}, bf16[128,2048]{0,1:T(8,128)(2,1)}, u32[]{:S(2)}) copy-start(bf16[128,2048]{0,1:T(8,128)(2,1)} %copy-done.2) | copy-start | bytes 1572868
  508.2 6.4 %copy-start.1 = (bf16[128,8,8,128]{3,0,2,1:T(8,128)(2,1)S(1)}, bf16[128,8,8,128]{3,0,2,1:T(8,128)(2,1)}, u32[]{:S(2)}) copy-start(bf16[128,8,8,128]{3,0,2,1:T(8,128)(2,1)} %copy.138) | copy-start | bytes 6291460
  521.9 5.7 copy-start
  546.4 5.7 copy-start
Sparse Core Ops, SparseCore 0:
  9.0 350.6 all-gather.2
where the time goes:
time: 589 us; the launch traced here: 581 us
  blocking collectives  292 us (50%)
  matrix products  81.7 us (14%)
  waiting for transfers between devices  57.2 us (10%)
  starting transfers between devices  55 us (9%)
  local copies, waits for them, and re-layouts  41.4 us (7%)
  other arithmetic  31.8 us (5%)
  between operations  18.9 us (3%)
    all_gather x1, blocking collectives, on_device(): plan = lax.all_gather(tile_plan, ('prompt', 'resp'), axis=0, tiled=True)  292 us
    dot_general x10, matrix products, absorb(): jnp.einsum('luem,mut->luet', attention_weight.astype(jnp.bfloat16), value...  65.2 us
    ppermute x14, waiting for transfers between devices, passed_along(): lax.ppermute(value, axis, [(source, source + steps) for source in range(f...  56.4 us
    ppermute x14, starting transfers between devices, passed_along(): lax.ppermute(value, axis, [(source, source + steps) for source in range(f...  55 us
    reduce_sum x10, other arithmetic, absorb(): total = total * factor + jnp.sum(attention_weight, axis=-1)  21.7 us
    dot_general x10, matrix products, absorb(): jnp.einsum('wcpo,lco->wcpl', query_head_rows, key_vectors, preferred_elem...  16.5 us
  transfers between devices with their start and end apart: 15, of which 7 were waited for; matrix products, arithmetic and copies ran while one was open for 14% of the time, Pallas kernels for 0%

commit v1 on v0

--- a/solution.py
+++ b/solution.py
@@ -91,7 +91,12 @@
     n_prompt = lax.axis_size("prompt")
     state = carry
     tiles = lax.all_gather(prefix_kv, ("prompt", "resp"), axis=0, tiled=True)
-    plan = lax.all_gather(tile_plan, ("prompt", "resp"), axis=0, tiled=True)
+    plan = jnp.concatenate(
+        lax.all_to_all(
+            jnp.stack([tile_plan] * lax.axis_size(("prompt", "resp"))), ("prompt", "resp"), 0, 0
+        ),
+        axis=0,
+    )
     count = tiles.shape[0]
     tile = tiles.shape[1]
     count = count // n_prompt

time: 589 us -> 485 us (0.82)
  the two profiles are of different devices: /device:TPU:89 before, /device:TPU:17 now
where the time goes in v1:
time: 485 us; the launch traced here: 477 us
  waiting for transfers between devices  266 us (55%)
  matrix products  66.8 us (14%)
  starting transfers between devices  48.4 us (10%)
  local copies, waits for them, and re-layouts  43.4 us (9%)
  other arithmetic  30.7 us (6%)
  between operations  19 us (4%)
    all_gather x1, waiting for transfers between devices, on_device(): tiles = lax.all_gather(prefix_kv, ('prompt', 'resp'), axis=0, tiled=True)  178 us
    ppermute x14, waiting for transfers between devices, passed_along(): lax.ppermute(value, axis, [(source, source + steps) for source in range(f...  86.8 us
    dot_general x8, matrix products, absorb(): jnp.einsum('luem,mut->luet', attention_weight.astype(jnp.bfloat16), value...  53.1 us
    ppermute x14, starting transfers between devices, passed_along(): lax.ppermute(value, axis, [(source, source + steps) for source in range(f...  30.7 us
    all_to_all x1, starting transfers between devices, on_device(): lax.all_to_all(jnp.stack([tile_plan] * lax.axis_size(('prompt', 'resp')))...  17.7 us
    reduce_sum x8, other arithmetic, absorb(): total = total * factor + jnp.sum(attention_weight, axis=-1)  17.2 us
    dot_general x8, matrix products, absorb(): jnp.einsum('wcpo,lco->wcpl', query_head_rows, key_vectors, preferred_elem...  13.7 us
  transfers between devices with their start and end apart: 16, of which 11 were waited for; matrix products, arithmetic and copies ran while one was open for 14% of the time, Pallas kernels for 0%

profile of v1, /device:TPU:17, one launch (start us, length us, event | category | flops | bytes accessed | tf_op | source)
XLA Modules:
  0.0 476.7 jit_solution(2891109789438799764)
XLA Ops:
  12.1 14.2 %collective-permute-done.7 = bf16[128,2048]{0,1:T(8,128)(2,1)S(1)} collective-permute-done((bf16[128,2048]{0,1:T(8,128)(2,1)S(1)}, bf16[128,2048]{0,1:T(8,128)(2,1)S(1)}, u32[]{:S(2)}, u32[]{:S(2)}) %collective-permute-start.7) | collective-permute-done | bytes 524320 | tf_op jit(solution)/shard_map/ppermute | solution.py:16
  28.2 15.0 %collective-permute-done.8 = bf16[128,2048]{0,1:T(8,128)(2,1)} collective-permute-done((bf16[128,2048]{0,1:T(8,128)(2,1)S(1)}, bf16[128,2048]{0,1:T(8,128)(2,1)}, u32[]{:S(2)}, u32[]{:S(2)}) %collective-permute-start.8) | collective-permute-done | bytes 524320 | tf_op jit(solution)/shard_map/ppermute | solution.py:16
  47.8 11.6 %collective-permute-done = s32[128]{0:T(128)S(1)} collective-permute-done((s32[128]{0:T(128)S(1)}, s32[128]{0:T(128)S(1)}, u32[]{:S(2)}, u32[]{:S(2)}) %collective-permute-start) | collective-permute-done | bytes 544 | tf_op jit(solution)/shard_map/ppermute | solution.py:16
  61.3 5.4 %collective-permute-done.1 = s32[128]{0:T(128)S(1)} collective-permute-done((s32[128]{0:T(128)S(1)}, s32[128]{0:T(128)S(1)}, u32[]{:S(2)}, u32[]{:S(2)}) %collective-permute-start.1) | collective-permute-done | bytes 544 | tf_op jit(solution)/shard_map/ppermute | solution.py:16
  68.6 5.4 %collective-permute-done.2 = s32[128]{0:T(128)S(1)} collective-permute-done((s32[128]{0:T(128)S(1)}, s32[128]{0:T(128)S(1)}, u32[]{:S(2)}, u32[]{:S(2)}) %collective-permute-start.2) | collective-permute-done | bytes 544 | tf_op jit(solution)/shard_map/ppermute | solution.py:16
  75.9 5.4 %collective-permute-done.3 = s32[128]{0:T(128)S(1)} collective-permute-done((s32[128]{0:T(128)S(1)}, s32[128]{0:T(128)S(1)}, u32[]{:S(2)}, u32[]{:S(2)}) %collective-permute-start.3) | collective-permute-done | bytes 544 | tf_op jit(solution)/shard_map/ppermute | solution.py:16
  84.6 17.7 %all-to-all-start = ((s32[128,4,2]{1,2,0:T(2,128)}), s32[128,4,2]{1,2,0:T(2,128)S(1)}, u32[]{:S(2)}, u32[]{:S(2)}) async-start(s32[128,4,2]{1,2,0:T(2,128)} %stack.2), calls=%async_computation | async-start | bytes 262144 | tf_op jit(solution)/shard_map/all_to_all | solution.py:95
  123.2 13.9 %collective-permute-done.10 = bf16[128,2048]{0,1:T(8,128)(2,1)S(1)} collective-permute-done((bf16[128,2048]{0,1:T(8,128)(2,1)S(1)}, bf16[128,2048]{0,1:T(8,128)(2,1)S(1)}, u32[]{:S(2)}, u32[]{:S(2)}) %collective-permute-start.10) | collective-permute-done | bytes 524320 | tf_op jit(solution)/shard_map/ppermute | solution.py:16
  140.3 12.6 %collective-permute-done.11 = bf16[128,2048]{0,1:T(8,128)(2,1)} collective-permute-done((bf16[128,2048]{0,1:T(8,128)(2,1)S(1)}, bf16[128,2048]{0,1:T(8,128)(2,1)}, u32[]{:S(2)}, u32[]{:S(2)}) %collective-permute-start.11) | collective-permute-done | bytes 524320 | tf_op jit(solution)/shard_map/ppermute | solution.py:16
  174.6 9.1 %conditional.8 = ((f32[128,8,8]{0,2,1:T(8,128)S(1)}, f32[128,8,8]{0,2,1:T(8,128)S(1)}, f32[128,8,8,128]{3,0,2,1:T(8,128)})) conditional(s32[]{:T(128)} %convert_element_type.71, (f32[128,8,8]{0,2,1:T(8,128)S(1)}, f32[128,8,8]{0,2,1:T(8,128)S(1)}, f32[128,8,8,128]{3,0,2,1:T(8,128)}) %tuple.61, (pred[128,128]{0,1:T(8,128)(4,1)}, ...), branch_computations={%region_9.10_spmd, %region_10.13_spmd} | conditional | flops 552615936 | bytes 25280572 | solution.py:88
  183.8 8.9 %conditional.9 = ((f32[128,8,8]{0,2,1:T(8,128)S(1)}, f32[128,8,8]{0,2,1:T(8,128)S(1)}, f32[128,8,8,128]{3,0,2,1:T(8,128)})) conditional(s32[]{:T(128)} %convert_element_type.70, (f32[128,8,8]{0,2,1:T(8,128)S(1)}, f32[128,8,8]{0,2,1:T(8,128)S(1)}, f32[128,8,8,128]{3,0,2,1:T(8,128)}) %get-tuple-element.662, (pred[128,128]{0,1:T(8,128)(4,1)S(1)}, ...), branch_computations={%region_13.14_spmd, %region_14.17_spmd} | conditional | flops 552615936 | bytes 25215008 | solution.py:88
  192.7 7.4 %conditional.10 = ((f32[128,8,8]{0,2,1:T(8,128)S(1)}, f32[128,8,8]{0,2,1:T(8,128)S(1)}, f32[128,8,8,128]{3,0,2,1:T(8,128)})) conditional(s32[]{:T(128)} %convert_element_type.69, (f32[128,8,8]{0,2,1:T(8,128)S(1)}, f32[128,8,8]{0,2,1:T(8,128)S(1)}, f32[128,8,8,128]{3,0,2,1:T(8,128)}) %get-tuple-element.663, (pred[128,128]{0,1:T(8,128)(4,1)S(1)}, ...), branch_computations={%region_17.18_spmd, %region_18.21_spmd} | conditional | flops 552615936 | bytes 25215008 | solution.py:88
  200.0 8.4 %conditional.11 = ((f32[128,8,8]{0,2,1:T(8,128)S(1)}, f32[128,8,8]{0,2,1:T(8,128)S(1)}, f32[128,8,8,128]{3,0,2,1:T(8,128)})) conditional(s32[]{:T(128)} %convert_element_type.68, (f32[128,8,8]{0,2,1:T(8,128)S(1)}, f32[128,8,8]{0,2,1:T(8,128)S(1)}, f32[128,8,8,128]{3,0,2,1:T(8,128)}) %get-tuple-element.664, (pred[128,128]{0,1:T(8,128)(4,1)S(1)}, ...), branch_computations={%region_21.0_spmd, %region_22.25_spmd} | conditional | flops 552615936 | bytes 25215008 | solution.py:88
  203.2 5.3 %bitcast_add_fusion.3 = f32[128,8,8,128]{3,0,2,1:T(8,128)} fusion(f32[128,8,8,128]{3,0,2,1:T(8,128)} %get-tuple-element.220, bf16[128,8,128,1]{0,2,3,1:T(8,128)(2,1)S(1)} %bitcast.269, f32[8,128,128,8]{2,1,3,0:T(8,128)S(1)} %get-tuple-element.506, f32[128,8,8]{0,2,1:T(8,128)S(1)} %get-tuple-element.480, f32[128,8,8]{0,2,1:T(8,128)S(1)} %max.20, ...), kind=kOutput, calls=%fused_computation.50 | convolution fusion | flops 275775488 | bytes 12926976 | tf_op jit(solution)/shard_map/cond/branch_1_fun/luem,mut->luet/dot_general | solution.py:32
  208.4 8.6 %conditional.12 = ((f32[128,8,8]{0,2,1:T(8,128)S(1)}, f32[128,8,8]{0,2,1:T(8,128)S(1)}, f32[128,8,8,128]{3,0,2,1:T(8,128)})) conditional(s32[]{:T(128)} %convert_element_type.67, (f32[128,8,8]{0,2,1:T(8,128)S(1)}, f32[128,8,8]{0,2,1:T(8,128)S(1)}, f32[128,8,8,128]{3,0,2,1:T(8,128)}) %get-tuple-element.665, (pred[128,128]{0,1:T(8,128)(4,1)S(1)}, ...), branch_computations={%region_25.0_spmd, %region_26.29_spmd} | conditional | flops 552615936 | bytes 25215008 | solution.py:88
  211.8 5.2 %bitcast_add_fusion.4 = f32[128,8,8,128]{3,0,2,1:T(8,128)} fusion(f32[128,8,8,128]{3,0,2,1:T(8,128)} %get-tuple-element.226, bf16[128,8,128,1]{0,2,3,1:T(8,128)(2,1)S(1)} %bitcast.270, f32[8,128,128,8]{2,1,3,0:T(8,128)S(1)} %get-tuple-element.510, f32[128,8,8]{0,2,1:T(8,128)S(1)} %get-tuple-element.482, f32[128,8,8]{0,2,1:T(8,128)S(1)} %max.21, ...), kind=kOutput, calls=%fused_computation.66 | convolution fusion | flops 275775488 | bytes 12926976 | tf_op jit(solution)/shard_map/cond/branch_1_fun/luem,mut->luet/dot_general | solution.py:32
  217.3 178.4 %all-gather.2.cloned.1.call-done = bf16[512,8,2048]{2,1,0:T(8,128)(2,1)} async-done(((bf16[4,8,2048]{2,1,0:T(8,128)(2,1)}), bf16[512,8,2048]{2,1,0:T(8,128)(2,1)}) %all-gather.2.cloned.1.call-update) | async-done | bytes 16777232 | tf_op jit(solution)/shard_map/all_gather | solution.py:93
  395.7 8.7 %gather_fusion.1 = bf16[128,8,2048]{2,1,0:T(8,128)(2,1)} fusion(bf16[512,8,2048]{2,1,0:T(8,128)(2,1)} %all-gather.2.cloned.1.call-done, s32[1024]{0:T(1024)} %pad_clamp_fusion), kind=kCustom, calls=%fused_computation.1 | custom fusion | bytes 8389120 | tf_op jit(solution)/shard_map/gather | solution.py:104
  404.4 6.4 %copy.137 = bf16[2,512,2048]{1,2,0:T(8,128)(2,1)} copy(bf16[2,512,2048]{2,1,0:T(8,128)(2,1)} %bitcast.260) | data formatting | bytes 8388608 | tf_op jit(solution)/shard_map/while | solution.py:129
  410.8 49.1 %while.14 = (s32[]{:T(128)}, f32[128,8,8]{0,2,1:T(8,128)S(1)}, f32[128,8,8]{0,2,1:T(8,128)S(1)}, f32[128,8,8,128]{3,0,2,1:T(8,128)}, pred[2,512]{1,0:T(4,128)(4,...) while((s32[]{:T(128)}, f32[128,8,8]{0,2,1:T(8,128)S(1)}, ...), condition=%wide.region_44.45_spmd, body=%wide.region_38.44_spmd.sunk | while | flops 2204123648 | bytes 138940144 | solution.py:129
  412.1 23.2 %conditional.16 = ((f32[128,8,8]{0,2,1:T(8,128)S(1)}, f32[128,8,8]{0,2,1:T(8,128)S(1)}, f32[128,8,8,128]{3,0,2,1:T(8,128)})) conditional(s32[]{:T(128)} %convert_element_type.97, (f32[128,8,8]{0,2,1:T(8,128)S(1)}, f32[128,8,8]{0,2,1:T(8,128)S(1)}, f32[128,8,8,128]{3,0,2,1:T(8,128)}) %tuple.148, (pred[1,512]{1,0:T(4,128)(4,1)S(1)}, ...), branch_computations={%region_40.40_spmd, %region_41.43_spmd} | conditional | flops 2204123136 | bytes 138938944 | solution.py:127
  423.8 11.5 %bitcast_add_fusion.7 = f32[128,8,8,128]{3,0,2,1:T(8,128)} fusion(f32[128,8,8,128]{3,0,2,1:T(8,128)} %get-tuple-element.245, bf16[512,8,128,1]{0,2,3,1:T(8,128)(2,1)S(1)} %bitcast.259, f32[8,512,128,8]{2,1,3,0:T(8,128)} %copy-done, f32[128,8,8]{0,2,1:T(8,128)S(1)} %max.24, pred[512]{0:T(512)(128)(4,1)S(1)} %reduce.1, f32[128,8,8]{0,2,1:T(8,128)S(1)} %get-tuple-element.488), kind=kOutput, calls=%fused_computation.124 | convolution fusion | flops 1096810496 | bytes 26280448 | tf_op jit(solution)/shard_map/while/body/eval_jaxpr/cond/branch_1_fun/luem,mut->luet/dot_general | solution.py:32
  436.6 23.2 %conditional.16 = ((f32[128,8,8]{0,2,1:T(8,128)S(1)}, f32[128,8,8]{0,2,1:T(8,128)S(1)}, f32[128,8,8,128]{3,0,2,1:T(8,128)})) conditional(s32[]{:T(128)} %convert_element_type.97, (f32[128,8,8]{0,2,1:T(8,128)S(1)}, f32[128,8,8]{0,2,1:T(8,128)S(1)}, f32[128,8,8,128]{3,0,2,1:T(8,128)}) %tuple.148, (pred[1,512]{1,0:T(4,128)(4,1)S(1)}, ...), branch_computations={%region_40.40_spmd, %region_41.43_spmd} | conditional | flops 2204123136 | bytes 138938944 | solution.py:127
  448.4 11.5 %bitcast_add_fusion.7 = f32[128,8,8,128]{3,0,2,1:T(8,128)} fusion(f32[128,8,8,128]{3,0,2,1:T(8,128)} %get-tuple-element.245, bf16[512,8,128,1]{0,2,3,1:T(8,128)(2,1)S(1)} %bitcast.259, f32[8,512,128,8]{2,1,3,0:T(8,128)} %copy-done, f32[128,8,8]{0,2,1:T(8,128)S(1)} %max.24, pred[512]{0:T(512)(128)(4,1)S(1)} %reduce.1, f32[128,8,8]{0,2,1:T(8,128)S(1)} %get-tuple-element.488), kind=kOutput, calls=%fused_computation.124 | convolution fusion | flops 1096810496 | bytes 26280448 | tf_op jit(solution)/shard_map/while/body/eval_jaxpr/cond/branch_1_fun/luem,mut->luet/dot_general | solution.py:32
  (119 shorter events, 127.2 us)
Async XLA Ops:
  6.5 389.2 %all-gather.2.cloned.1.call-start = ((), (), s32[]{:S(2)}) async-start(), calls=%async_computation.1 | async-start | bytes 16908288 | tf_op jit(solution)/shard_map/all_gather | solution.py:93
  8.6 17.8 %collective-permute-start.7 = (bf16[128,2048]{0,1:T(8,128)(2,1)S(1)}, bf16[128,2048]{0,1:T(8,128)(2,1)S(1)}, u32[]{:S(2)}, u32[]{:S(2)}) collective-permute-start(bf16[128,2048]{0,1:T(8,128)(2,1)S(1)} %bitcast.263), channel_id=1, source_target_pairs={{0,1},{1,2},{2,3},{3,4},{4,5},{5,6},{6,7},{7,8},{8,9},{9,10},{10,1... | collective-permute-start | bytes 1572872 | tf_op jit(solution)/shard_map/ppermute | solution.py:16
  26.3 79.3 %copy-start.3 = (bf16[128,2048]{0,1:T(8,128)(2,1)}, bf16[128,2048]{0,1:T(8,128)(2,1)S(1)}, u32[]{:S(2)}) copy-start(bf16[128,2048]{0,1:T(8,128)(2,1)S(1)} %collective-permute-done.7) | copy-start | bytes 1572868
  26.3 16.9 %collective-permute-start.8 = (bf16[128,2048]{0,1:T(8,128)(2,1)S(1)}, bf16[128,2048]{0,1:T(8,128)(2,1)}, u32[]{:S(2)}, u32[]{:S(2)}) collective-permute-start(bf16[128,2048]{0,1:T(8,128)(2,1)S(1)} %collective-permute-done.7), channel_id=1, source_target_pairs={{0,1},{1,2},{2,3},{3,4},{4,5},{5,6},{6,7},{7,8},{8,9},{9,10},{10,1... | collective-permute-start | bytes 1572872 | tf_op jit(solution)/shard_map/ppermute | solution.py:16
  43.3 77.2 %collective-permute-start.9 = (bf16[128,2048]{0,1:T(8,128)(2,1)}, bf16[128,2048]{0,1:T(8,128)(2,1)S(1)}, u32[]{:S(2)}, u32[]{:S(2)}) collective-permute-start(bf16[128,2048]{0,1:T(8,128)(2,1)} %collective-permute-done.8), channel_id=1, source_target_pairs={{0,1},{1,2},{2,3},{3,4},{4,5},{5,6},{6,7},{7,8},{8,9},{9,10},{10,1... | collective-permute-start | bytes 1572872 | tf_op jit(solution)/shard_map/ppermute | solution.py:16
  45.8 13.6 %collective-permute-start = (s32[128]{0:T(128)S(1)}, s32[128]{0:T(128)S(1)}, u32[]{:S(2)}, u32[]{:S(2)}) collective-permute-start(s32[128]{0:T(128)S(1)} %add_bitcast_fusion), channel_id=1, source_target_pairs={{0,1},{1,2},{2,3},{3,4},{4,5},{5,6},{6,7},{7,8},{8,9},{9,10},{10,1... | collective-permute-start | bytes 1544 | tf_op jit(solution)/shard_map/ppermute | solution.py:16
  59.4 7.3 %collective-permute-start.1 = (s32[128]{0:T(128)S(1)}, s32[128]{0:T(128)S(1)}, u32[]{:S(2)}, u32[]{:S(2)}) collective-permute-start(s32[128]{0:T(128)S(1)} %collective-permute-done), channel_id=1, source_target_pairs={{0,1},{1,2},{2,3},{3,4},{4,5},{5,6},{6,7},{7,8},{8,9},{9,10},{10,1... | collective-permute-start | bytes 1544 | tf_op jit(solution)/shard_map/ppermute | solution.py:16
  66.7 7.3 %collective-permute-start.2 = (s32[128]{0:T(128)S(1)}, s32[128]{0:T(128)S(1)}, u32[]{:S(2)}, u32[]{:S(2)}) collective-permute-start(s32[128]{0:T(128)S(1)} %collective-permute-done.1), channel_id=1, source_target_pairs={{0,1},{1,2},{2,3},{3,4},{4,5},{5,6},{6,7},{7,8},{8,9},{9,10},{10,1... | collective-permute-start | bytes 1544 | tf_op jit(solution)/shard_map/ppermute | solution.py:16
  74.0 7.3 %collective-permute-start.3 = (s32[128]{0:T(128)S(1)}, s32[128]{0:T(128)S(1)}, u32[]{:S(2)}, u32[]{:S(2)}) collective-permute-start(s32[128]{0:T(128)S(1)} %collective-permute-done.2), channel_id=1, source_target_pairs={{0,1},{1,2},{2,3},{3,4},{4,5},{5,6},{6,7},{7,8},{8,9},{9,10},{10,1... | collective-permute-start | bytes 1544 | tf_op jit(solution)/shard_map/ppermute | solution.py:16
  81.3 20.9 %collective-permute-start.4 = (s32[128]{0:T(128)S(1)}, s32[128]{0:T(128)S(1)}, u32[]{:S(2)}, u32[]{:S(2)}) collective-permute-start(s32[128]{0:T(128)S(1)} %collective-permute-done.3), channel_id=1, source_target_pairs={{0,1},{1,2},{2,3},{3,4},{4,5},{5,6},{6,7},{7,8},{8,9},{9,10},{10,1... | collective-permute-start | bytes 1544 | tf_op jit(solution)/shard_map/ppermute | solution.py:16
  84.6 78.6 %all-to-all-start = ((s32[128,4,2]{1,2,0:T(2,128)}), s32[128,4,2]{1,2,0:T(2,128)S(1)}, u32[]{:S(2)}, u32[]{:S(2)}) async-start(s32[128,4,2]{1,2,0:T(2,128)} %stack.2), calls=%async_computation | async-start | bytes 262144 | tf_op jit(solution)/shard_map/all_to_all | solution.py:95
  102.3 9.2 %collective-permute-start.5 = (s32[128]{0:T(128)S(1)}, s32[128]{0:T(128)S(1)}, u32[]{:S(2)}, u32[]{:S(2)}) collective-permute-start(s32[128]{0:T(128)S(1)} %collective-permute-done.4), channel_id=1, source_target_pairs={{0,1},{1,2},{2,3},{3,4},{4,5},{5,6},{6,7},{7,8},{8,9},{9,10},{10,1... | collective-permute-start | bytes 1544 | tf_op jit(solution)/shard_map/ppermute | solution.py:16
  111.5 7.3 %collective-permute-start.6 = (s32[128]{0:T(128)S(1)}, s32[128]{0:T(128)S(1)}, u32[]{:S(2)}, u32[]{:S(2)}) collective-permute-start(s32[128]{0:T(128)S(1)} %collective-permute-done.5), channel_id=1, source_target_pairs={{0,1},{1,2},{2,3},{3,4},{4,5},{5,6},{6,7},{7,8},{8,9},{9,10},{10,1... | collective-permute-start | bytes 1544 | tf_op jit(solution)/shard_map/ppermute | solution.py:16
  120.4 16.6 %collective-permute-start.10 = (bf16[128,2048]{0,1:T(8,128)(2,1)S(1)}, bf16[128,2048]{0,1:T(8,128)(2,1)S(1)}, u32[]{:S(2)}, u32[]{:S(2)}) collective-permute-start(bf16[128,2048]{0,1:T(8,128)(2,1)S(1)} %collective-permute-done.9), channel_id=1, source_target_pairs={{0,1},{1,2},{2,3},{3,4},{4,5},{5,6},{6,7},{7,8},{8,9},{9,10},{10,1... | collective-permute-start | bytes 1572872 | tf_op jit(solution)/shard_map/ppermute | solution.py:16
  137.1 21.7 %copy-start.2 = (bf16[128,2048]{0,1:T(8,128)(2,1)}, bf16[128,2048]{0,1:T(8,128)(2,1)S(1)}, u32[]{:S(2)}) copy-start(bf16[128,2048]{0,1:T(8,128)(2,1)S(1)} %collective-permute-done.10) | copy-start | bytes 1572868
  137.1 15.9 %collective-permute-start.11 = (bf16[128,2048]{0,1:T(8,128)(2,1)S(1)}, bf16[128,2048]{0,1:T(8,128)(2,1)}, u32[]{:S(2)}, u32[]{:S(2)}) collective-permute-start(bf16[128,2048]{0,1:T(8,128)(2,1)S(1)} %collective-permute-done.10), channel_id=1, source_target_pairs={{0,1},{1,2},{2,3},{3,4},{4,5},{5,6},{6,7},{7,8},{8,9},{9,10},{10,1... | collective-permute-start | bytes 1572872 | tf_op jit(solution)/shard_map/ppermute | solution.py:16
  152.9 15.2 %collective-permute-start.12 = (bf16[128,2048]{0,1:T(8,128)(2,1)}, bf16[128,2048]{0,1:T(8,128)(2,1)}, u32[]{:S(2)}, u32[]{:S(2)}) collective-permute-start(bf16[128,2048]{0,1:T(8,128)(2,1)} %collective-permute-done.11), channel_id=1, source_target_pairs={{0,1},{1,2},{2,3},{3,4},{4,5},{5,6},{6,7},{7,8},{8,9},{9,10},{10,1... | collective-permute-start | bytes 1572872 | tf_op jit(solution)/shard_map/ppermute | solution.py:16
  168.1 48.9 %collective-permute-start.13 = (bf16[128,2048]{0,1:T(8,128)(2,1)}, bf16[128,2048]{0,1:T(8,128)(2,1)S(1)}, u32[]{:S(2)}, u32[]{:S(2)}) collective-permute-start(bf16[128,2048]{0,1:T(8,128)(2,1)} %collective-permute-done.12), channel_id=1, source_target_pairs={{0,1},{1,2},{2,3},{3,4},{4,5},{5,6},{6,7},{7,8},{8,9},{9,10},{10,1... | collective-permute-start | bytes 1572872 | tf_op jit(solution)/shard_map/ppermute | solution.py:16
  174.6 9.1 %copy-start.4 = (pred[128,128]{0,1:T(8,128)(4,1)S(1)}, pred[128,128]{0,1:T(8,128)(4,1)}, u32[]{:S(2)}) copy-start(pred[128,128]{0,1:T(8,128)(4,1)} %get-tuple-element.532) | copy-start | bytes 49156
  174.7 2.6 copy-start.5
  404.4 6.4 %copy-start.1 = (bf16[128,8,8,128]{3,0,2,1:T(8,128)(2,1)S(1)}, bf16[128,8,8,128]{3,0,2,1:T(8,128)(2,1)}, u32[]{:S(2)}) copy-start(bf16[128,8,8,128]{3,0,2,1:T(8,128)(2,1)} %copy.138) | copy-start | bytes 6291460
  418.1 5.7 %copy-start = (f32[8,512,128,8]{2,1,3,0:T(8,128)}, f32[8,512,128,8]{2,1,3,0:T(8,128)S(1)}, u32[]{:S(2)}) copy-start(f32[8,512,128,8]{2,1,3,0:T(8,128)S(1)} %get-tuple-element.522) | copy-start | bytes 50331652 | tf_op jit(solution)/shard_map/while/body/eval_jaxpr/cond
  442.6 5.7 %copy-start = (f32[8,512,128,8]{2,1,3,0:T(8,128)}, f32[8,512,128,8]{2,1,3,0:T(8,128)S(1)}, u32[]{:S(2)}) copy-start(f32[8,512,128,8]{2,1,3,0:T(8,128)S(1)} %get-tuple-element.522) | copy-start | bytes 50331652 | tf_op jit(solution)/shard_map/while/body/eval_jaxpr/cond
Sparse Core Ops, SparseCore 0:
  9.0 386.6 all-gather.1
